TPU v7x, 512 devices: a whole 4x8x8 slice. The times are simulated.
512 devices in a mesh: ctx: 64 (over z_lo, y, core), head: 8 (over z_hi, x).
Axes of the slice: x: 4, y: 8, z: 8 (z_hi: 2, z_lo: 4; z = z_hi * 4 + z_lo), core: 2. Of those that a mesh axis runs over, the one named last changes fastest.
Arguments:
- frozen_queries: bfloat16 [8192, 12288], P('ctx', 'head'), may hold values from -20.4 to 20.4
- query_latent_rows: bfloat16 [8192, 1536], P('ctx'), may hold values from -6 to 6
- key_value_latent: bfloat16 [8192, 576], P('ctx'), may hold values from -20.4 to 20.4
- block_starts: int32 [64, 2], P('ctx'), may hold values from 0 to 960, as said below
- latent_up_weight: bfloat16 [512, 16384], P(None, 'head'), may hold values from -0.25 to 0.25
- query_adapter_first: bfloat16 [1536, 32], replicated, may hold values from -0.15625 to 0.15625
- query_adapter_second: bfloat16 [32, 12288], P(None, 'head'), may hold values from -1 to 1
- output_adapter_first: bfloat16 [8192, 32], P('head'), may hold values from -0.0625 to 0.0625
- output_adapter_second: bfloat16 [32, 2560], replicated, may hold values from -1 to 1
- frozen_output_weight: bfloat16 [8192, 2560], P('head', 'ctx'), may hold values from -0.0625 to 0.0625
- output_cotangent: bfloat16 [8192, 2560], P('ctx'), may hold values from -0.1875 to 0.1875
Outputs:
- grad_qa: float32 [1536, 32], replicated
- grad_qb: float32 [32, 12288], P(None, 'head')
- grad_oa: float32 [8192, 32], P('head')
- grad_ob: float32 [32, 2560], P(None, 'ctx')
Inputs may be any that keep to these rules, and one draw needn't show every extreme that they name: For c < 8, each of the 8 groups of one sequence holds block_starts = (c * 64, (15 - c) * 64), every c once per sequence.
All inputs are finite; a program needn't handle non-finite values.
Results may differ from a plain program's by a relative error of at most 0.02.
The roundings to bfloat16 on the way count: a program that leaves them out, or rounds other values in their place, can miss the bound.
Values may be sent and summed in bfloat16 or wider, within the bound.
A program may use at most 128 MiB of HBM per device.

v0:
```python
import jax
import jax.numpy as jnp
from jax import lax
from jax.sharding import PartitionSpec as P

PLAIN_WIDTH = 128
ROTARY_WIDTH = 64
VALUE_WIDTH = 128
KVL = 512
SPAN = 8
ROPE_BASE = 10000.0


def passed_along(value, axis, steps):
    count = lax.axis_size(axis)
    pairs = [(source, (source + steps) % count) for source in range(count)]
    return lax.ppermute(value, axis, pairs)


def rotate(vectors, positions, sign):
    half_width = vectors.shape[-1] // 2
    freq = ROPE_BASE ** (-jnp.arange(half_width, dtype=jnp.float32) * 2.0 / vectors.shape[-1])
    angle = positions.astype(jnp.float32)[..., None] * freq
    angle = angle.reshape(
        positions.shape + (1,) * (vectors.ndim - positions.ndim - 1) + (half_width,)
    )
    cosine = jnp.cos(angle)
    sine = jnp.sin(angle) * sign
    first = vectors[..., :half_width]
    second = vectors[..., half_width:]
    return jnp.concatenate([first * cosine - second * sine, second * cosine + first * sine], -1)


def block_positions(offsets, half_rows):
    steps = jnp.arange(half_rows, dtype=jnp.int32)
    return jnp.concatenate([offsets[0] + steps, offsets[1] + steps])


def expand_block(latent_rows, latent_up_weight, positions):
    kv_up = jnp.dot(
        latent_rows[:, :KVL], latent_up_weight, preferred_element_type=jnp.float32
    ).astype(jnp.bfloat16)
    rope_key = rotate(latent_rows[:, KVL:].astype(jnp.float32), positions, 1.0).astype(jnp.bfloat16)
    return jnp.concatenate([kv_up, rope_key], -1)


def block_scores(query_full, block, head_number):
    split = head_number * (PLAIN_WIDTH + VALUE_WIDTH)
    kv_heads = block[:, :split].reshape(block.shape[0], head_number, PLAIN_WIDTH + VALUE_WIDTH)
    nope_part = jnp.einsum(
        "qhd,khd->hqk",
        query_full[..., :PLAIN_WIDTH],
        kv_heads[..., :PLAIN_WIDTH],
        preferred_element_type=jnp.float32,
    )
    rope_part = jnp.einsum(
        "qhd,kd->hqk",
        query_full[..., PLAIN_WIDTH:],
        block[:, split:],
        preferred_element_type=jnp.float32,
    )
    return nope_part + rope_part


def contract_rows(left, right):
    return lax.dot_general(
        left, right, (((0,), (0,)), ((), ())), preferred_element_type=jnp.float32
    )


def columns_contract(left, right):
    return lax.dot_general(
        left, right, (((1,), (1,)), ((), ())), preferred_element_type=jnp.float32
    )


def body(
    frozen_queries,
    query_latent_rows,
    key_value_latent,
    block_starts,
    latent_up_weight,
    query_adapter_first,
    query_adapter_second,
    output_adapter_first,
    output_adapter_second,
    frozen_output_weight,
    output_cotangent,
):
    token_rows = frozen_queries.shape[0]
    half_rows = token_rows // 2
    per_head_width = PLAIN_WIDTH + ROTARY_WIDTH
    head_number = query_adapter_second.shape[1] // per_head_width
    score_scale = per_head_width ** (-0.5)
    axis_count = lax.axis_size("ctx")
    stride = axis_count // SPAN
    axis_place = lax.axis_index("ctx")
    all_offsets = lax.all_gather(block_starts, "ctx", axis=0, tiled=True)
    own_positions = block_positions(block_starts[0], half_rows)
    query_rank_rows = jnp.dot(
        query_latent_rows, query_adapter_first, preferred_element_type=jnp.float32
    ).astype(jnp.bfloat16)
    query_full = frozen_queries.astype(jnp.float32) + jnp.dot(
        query_rank_rows, query_adapter_second, preferred_element_type=jnp.float32
    )
    query_full = query_full.reshape(token_rows, head_number, per_head_width)
    query_full = jnp.concatenate(
        [query_full[..., :PLAIN_WIDTH], rotate(query_full[..., PLAIN_WIDTH:], own_positions, 1.0)],
        -1,
    ).astype(jnp.bfloat16)

    def prepare(block, positions):
        return expand_block(block, latent_up_weight, positions)

    collected = []

    def take(block, distance):
        source = (axis_place - distance * stride) % axis_count
        source_offsets = lax.dynamic_index_in_dim(all_offsets, source, 0, keepdims=False)
        positions = block_positions(source_offsets, half_rows)
        expanded = prepare(block, positions)
        collected.append((expanded, positions, block_scores(query_full, expanded, head_number)))

    take(key_value_latent, 0)
    moving = key_value_latent
    for hop in range(1, SPAN):
        moving = passed_along(moving, "ctx", stride)
        take(moving, hop)
    kv_all = jnp.concatenate([entry[0] for entry in collected], 0)
    key_positions = jnp.concatenate([entry[1] for entry in collected], 0)
    scores = jnp.concatenate([entry[2] for entry in collected], -1) * score_scale
    causal = key_positions[None, :] <= own_positions[:, None]
    scores = jnp.where(causal[None], scores, -jnp.inf)
    top = jnp.max(scores, -1, keepdims=True)
    expo = jnp.exp(scores - top)
    weights = (expo / jnp.sum(expo, -1, keepdims=True)).astype(jnp.bfloat16)
    split = head_number * (PLAIN_WIDTH + VALUE_WIDTH)
    key_count = kv_all.shape[0]
    kv_heads = kv_all[:, :split].reshape(key_count, head_number, PLAIN_WIDTH + VALUE_WIDTH)
    key_nope = kv_heads[..., :PLAIN_WIDTH]
    values = kv_heads[..., PLAIN_WIDTH:]
    rope_keys = kv_all[:, split:]
    attended_values = jnp.einsum(
        "hqk,khv->qhv", weights, values, preferred_element_type=jnp.float32
    ).astype(jnp.bfloat16)
    attended_flattened = attended_values.reshape(token_rows, head_number * VALUE_WIDTH)
    output_partial_sum = jnp.dot(
        attended_flattened, output_adapter_first, preferred_element_type=jnp.float32
    )
    output_rank_rows = lax.psum(output_partial_sum, "head").astype(jnp.bfloat16)
    output_rank_gradient = columns_contract(output_cotangent, output_adapter_second).astype(
        jnp.bfloat16
    )
    grad_ob = lax.psum_scatter(
        contract_rows(output_rank_rows, output_cotangent), "ctx", scatter_dimension=1, tiled=True
    )
    grad_oa = lax.psum(contract_rows(attended_flattened, output_rank_gradient), "ctx")
    frozen_query_gradient = columns_contract(
        output_cotangent, lax.all_gather(frozen_output_weight, "ctx", axis=1, tiled=True)
    )
    attended_gradient = (
        (frozen_query_gradient + columns_contract(output_rank_gradient, output_adapter_first))
        .astype(jnp.bfloat16)
        .reshape(token_rows, head_number, VALUE_WIDTH)
    )
    d_prob = jnp.einsum(
        "qhv,khv->hqk", attended_gradient, values, preferred_element_type=jnp.float32
    )
    weights_wide = weights.astype(jnp.float32)
    delta = jnp.sum(weights_wide * d_prob, -1, keepdims=True)
    d_score = (weights_wide * (d_prob - delta) * score_scale).astype(jnp.bfloat16)
    dq_nope = jnp.einsum("hqk,khd->qhd", d_score, key_nope, preferred_element_type=jnp.float32)
    dq_rope = jnp.einsum("hqk,kd->qhd", d_score, rope_keys, preferred_element_type=jnp.float32)
    dq_rope = rotate(dq_rope, own_positions, -1.0)
    query_gradient = (
        jnp.concatenate([dq_nope, dq_rope], -1)
        .reshape(token_rows, head_number * per_head_width)
        .astype(jnp.bfloat16)
    )
    qb_term = contract_rows(query_rank_rows, query_gradient)
    query_adapter_gradient = lax.psum(
        columns_contract(query_gradient, query_adapter_second), "head"
    ).astype(jnp.bfloat16)
    qa_term = contract_rows(query_latent_rows, query_adapter_gradient)
    grad_qb, grad_qa = lax.psum((qb_term, qa_term), "ctx")
    return (grad_qa, grad_qb, grad_oa, grad_ob)


def solution(mesh):
    return jax.shard_map(
        body,
        mesh=mesh,
        in_specs=(
            P("ctx", "head"),
            P("ctx", None),
            P("ctx", None),
            P("ctx", None),
            P(None, "head"),
            P(),
            P(None, "head"),
            P("head", None),
            P(),
            P("head", "ctx"),
            P("ctx", None),
        ),
        out_specs=(P(), P(None, "head"), P("head", None), P(None, "ctx")),
        check_vma=False,
    )
```

profile of v0, /device:TPU:1, one launch (start us, length us, event | category | flops | bytes accessed | tf_op | source)
XLA Modules:
  0.0 902.7 jit_solution(16338640068785759681)
XLA Ops:
  7.3 8.5 collective-permute-start
  24.4 80.7 %all-gather = s32[64,1,2]{2,1,0:T(1,128)} all-gather(s32[1,1,2]{2,1,0:T(1,128)S(1)} %bitcast.209), channel_id=1, replica_groups=mesh['ctx'=64,'head'=8] {'ctx'}, dimensions={0}, use_global_device_ids=true | all-gather | bytes 520 | tf_op jit(solution)/shard_map/all_gather | solution.py:98
  123.5 2.0 fusion.62
  145.4 1.9 constant_dynamic-update-slice_fusion.7
  150.6 2.0 constant_dynamic-update-slice_fusion.6
  152.6 1.9 collective-permute-start.1
  154.5 2.0 fusion.60
  156.5 10.0 %collective-permute-done.1 = bf16[128,576]{0,1:T(8,128)(2,1)S(1)} collective-permute-done((bf16[128,576]{0,1:T(8,128)(2,1)}, bf16[128,576]{0,1:T(8,128)(2,1)S(1)}, u32[]{:S(2)}, u32[]{:S(2)}) %collective-permute-start.1) | collective-permute-done | bytes 147488 | tf_op jit(solution)/shard_map/ppermute | solution.py:17
  168.2 1.9 collective-permute-start.2
  170.2 11.2 %collective-permute-done.2 = bf16[128,576]{0,1:T(8,128)(2,1)S(1)} collective-permute-done((bf16[128,576]{0,1:T(8,128)(2,1)S(1)}, bf16[128,576]{0,1:T(8,128)(2,1)S(1)}, u32[]{:S(2)}, u32[]{:S(2)}) %collective-permute-start.2) | collective-permute-done | bytes 147488 | tf_op jit(solution)/shard_map/ppermute | solution.py:17
  183.1 1.9 collective-permute-start.3
  185.0 11.9 %collective-permute-done.3 = bf16[128,576]{0,1:T(8,128)(2,1)S(1)} collective-permute-done((bf16[128,576]{0,1:T(8,128)(2,1)S(1)}, bf16[128,576]{0,1:T(8,128)(2,1)S(1)}, u32[]{:S(2)}, u32[]{:S(2)}) %collective-permute-start.3) | collective-permute-done | bytes 147488 | tf_op jit(solution)/shard_map/ppermute | solution.py:17
  207.0 1.9 concatenate.151
  210.7 1.9 concatenate.155
  212.6 1.9 collective-permute-start.4
  214.5 1.9 constant_dynamic-update-slice_fusion.5
  216.5 1.9 constant_dynamic-update-slice_fusion.4
  218.4 1.9 constant_dynamic-update-slice_fusion.3
  220.3 1.9 fusion.54
  222.3 3.1 collective-permute-done.4
  226.0 1.9 collective-permute-start.5
  228.9 10.8 %collective-permute-done.5 = bf16[128,576]{0,1:T(8,128)(2,1)S(1)} collective-permute-done((bf16[128,576]{0,1:T(8,128)(2,1)S(1)}, bf16[128,576]{0,1:T(8,128)(2,1)S(1)}, u32[]{:S(2)}, u32[]{:S(2)}) %collective-permute-start.5) | collective-permute-done | bytes 147488 | tf_op jit(solution)/shard_map/ppermute | solution.py:17
  240.4 1.9 collective-permute-start.6
  243.4 9.6 %collective-permute-done.6 = bf16[128,576]{0,1:T(8,128)(2,1)S(1)} collective-permute-done((bf16[128,576]{0,1:T(8,128)(2,1)S(1)}, bf16[128,576]{0,1:T(8,128)(2,1)S(1)}, u32[]{:S(2)}, u32[]{:S(2)}) %collective-permute-start.6) | collective-permute-done | bytes 147488 | tf_op jit(solution)/shard_map/ppermute | solution.py:17
  262.6 2.5 slice.337
  271.0 1.9 fusion.188
  277.3 3.3 fusion.197
  280.9 2.7 fusion.16
  283.6 6.7 fusion.42
  290.4 7.4 fusion.43
  300.0 50.8 %all-reduce.2 = (bf16[128,32]{0,1:T(8,128)(2,1)S(1)}, bf16[128,32]{0,1:T(8,128)(2,1)S(1)}) all-reduce(f32[128,32]{0,1:T(8,128)S(1)} %fusion.200, f32[128,32]{0,1:T(8,128)} %fusion.201), channel_id=1, replica_groups=mesh['ctx'=64,'head'=8] {'head'}, use_global_device_ids=true, to_apply=%region_3.4 | all-reduce | flops 8192 | bytes 49152 | tf_op jit(solution)/shard_map/psum | solution.py:181
  354.6 535.1 %all-reduce.5.cloned.1.call-done = (f32[1536,32]{0,1:T(8,128)}, f32[32,1536]{1,0:T(8,128)}, f32[1024,32]{0,1:T(8,128)}, f32[32,2560]{1,0:T(8,128)}) async-done(((f32[1536,32]{0,1:T(8,128)}, f32[32,1536]{1,0:T(8,128)}, f32[1024,32]{0,1:T(8,128)}, f32[32,2560]{1,0:T(8,128)}), (f32[1536,32]{0,1:T(8,128)}, f32[32,1536]{1,0:T(8,128)}, f32[1024,32]{0,1:T(8,128)}, ...) | async-done | bytes 851984 | tf_op jit(solution)/shard_map/psum | solution.py:185
  (297 shorter events, 99.3 us)
Async XLA Ops:
  7.2 16.6 %copy-start.62 = (s32[1,2]{1,0:T(1,128)S(1)}, s32[1,2]{1,0:T(1,128)}, u32[]{:S(2)}) copy-start(s32[1,2]{1,0:T(1,128)} %param.14) | copy-start | bytes 28
  7.2 270.1 %all-gather.3.cloned.1.call-start = ((), (), s32[]{:S(2)}) async-start(), calls=%async_computation | async-start | bytes 5324800 | tf_op jit(solution)/shard_map/all_gather | solution.py:159
  7.3 128.1 %collective-permute-start = (bf16[128,576]{0,1:T(8,128)(2,1)}, bf16[128,576]{0,1:T(8,128)(2,1)}, u32[]{:S(2)}, u32[]{:S(2)}) collective-permute-start(bf16[128,576]{0,1:T(8,128)(2,1)} %param.13), channel_id=1, source_target_pairs={{0,64},{8,72},{16,80},{24,88},{32,96},{40,104},{48,112},{56,120},{... | collective-permute-start | bytes 442376 | tf_op jit(solution)/shard_map/ppermute | solution.py:17
  15.8 873.8 %all-reduce.5.cloned.1.call-start = ((), (), s32[]{:S(2)}) async-start(), calls=%async_computation.1 | async-start | bytes 1703936 | tf_op jit(solution)/shard_map/psum | solution.py:185
  18.0 113.1 %copy-start.2 = (bf16[128,2560]{1,0:T(8,128)(2,1)S(1)}, bf16[128,2560]{1,0:T(8,128)(2,1)}, u32[]{:S(2)}) copy-start(bf16[128,2560]{1,0:T(8,128)(2,1)} %param.21) | copy-start | bytes 1966084
  109.0 19.7 %copy-start.70 = (s32[64]{0:T(128)}, s32[64]{0:T(128)S(1)}, u32[]{:S(2)}) copy-start(s32[64]{0:T(128)S(1)} %iota_add_fusion.14) | copy-start | bytes 772
  109.6 19.1 %copy-start.71 = (s32[64]{0:T(128)}, s32[64]{0:T(128)S(1)}, u32[]{:S(2)}) copy-start(s32[64]{0:T(128)S(1)} %iota_add_fusion.15) | copy-start | bytes 772
  110.9 17.8 %copy-start.78 = (s32[64]{0:T(128)}, s32[64]{0:T(128)S(1)}, u32[]{:S(2)}) copy-start(s32[64]{0:T(128)S(1)} %iota_add_fusion.2) | copy-start | bytes 772
  111.5 17.2 %copy-start.79 = (s32[64]{0:T(128)}, s32[64]{0:T(128)S(1)}, u32[]{:S(2)}) copy-start(s32[64]{0:T(128)S(1)} %iota_add_fusion.3) | copy-start | bytes 772
  112.8 15.9 %copy-start.72 = (s32[64]{0:T(128)}, s32[64]{0:T(128)S(1)}, u32[]{:S(2)}) copy-start(s32[64]{0:T(128)S(1)} %iota_add_fusion.6) | copy-start | bytes 772
  113.5 15.3 %copy-start.73 = (s32[64]{0:T(128)}, s32[64]{0:T(128)S(1)}, u32[]{:S(2)}) copy-start(s32[64]{0:T(128)S(1)} %iota_add_fusion.7) | copy-start | bytes 772
  140.7 26.3 %copy-start.32 = (bf16[128,32]{0,1:T(8,128)(2,1)}, bf16[128,32]{0,1:T(8,128)(2,1)S(1)}, u32[]{:S(2)}) copy-start(bf16[128,32]{0,1:T(8,128)(2,1)S(1)} %get-tuple-element.30) | copy-start | bytes 24580
  140.7 26.3 %copy-start.34 = (bf16[128,32]{0,1:T(8,128)(2,1)}, bf16[128,32]{0,1:T(8,128)(2,1)S(1)}, u32[]{:S(2)}) copy-start(bf16[128,32]{0,1:T(8,128)(2,1)S(1)} %get-tuple-element.31) | copy-start | bytes 24580
  152.6 13.9 %collective-permute-start.1 = (bf16[128,576]{0,1:T(8,128)(2,1)}, bf16[128,576]{0,1:T(8,128)(2,1)S(1)}, u32[]{:S(2)}, u32[]{:S(2)}) collective-permute-start(bf16[128,576]{0,1:T(8,128)(2,1)} %collective-permute-done), channel_id=1, source_target_pairs={{0,64},{8,72},{16,80},{24,88},{32,96},{40,104},{48,112},{56,120},{... | collective-permute-start | bytes 442376 | tf_op jit(solution)/shard_map/ppermute | solution.py:17
  167.0 16.1 %copy-start.5 = (bf16[128,2048]{1,0:T(8,128)(2,1)}, bf16[128,2048]{1,0:T(8,128)(2,1)S(1)}, u32[]{:S(2)}) copy-start(bf16[128,2048]{1,0:T(8,128)(2,1)S(1)} %convolution_convert_fusion.5) | copy-start | bytes 1572868
  168.2 13.1 %collective-permute-start.2 = (bf16[128,576]{0,1:T(8,128)(2,1)S(1)}, bf16[128,576]{0,1:T(8,128)(2,1)S(1)}, u32[]{:S(2)}, u32[]{:S(2)}) collective-permute-start(bf16[128,576]{0,1:T(8,128)(2,1)S(1)} %collective-permute-done.1), channel_id=1, source_target_pairs={{0,64},{8,72},{16,80},{24,88},{32,96},{40,104},{48,112},{56,120},{... | collective-permute-start | bytes 442376 | tf_op jit(solution)/shard_map/ppermute | solution.py:17
  181.8 17.1 %copy-start.60 = (f32[32]{0:T(128)S(1)}, f32[32]{0:T(128)}, u32[]{:S(2)}) copy-start(f32[32]{0:T(128)} %multiply_power_fusion) | copy-start | bytes 388
  181.8 17.1 %copy-start.66 = (f32[128]{0:T(128)S(1)}, f32[128]{0:T(128)}, u32[]{:S(2)}) copy-start(f32[128]{0:T(128)} %get-tuple-element.79) | copy-start | bytes 1540
  181.8 17.1 %copy-start.67 = (f32[128]{0:T(128)S(1)}, f32[128]{0:T(128)}, u32[]{:S(2)}) copy-start(f32[128]{0:T(128)} %get-tuple-element.80) | copy-start | bytes 1540
  181.9 17.1 %copy-start.77 = (f32[128]{0:T(128)S(1)}, f32[128]{0:T(128)}, u32[]{:S(2)}) copy-start(f32[128]{0:T(128)} %add_convert_fusion.6) | copy-start | bytes 1540
  183.1 13.8 %collective-permute-start.3 = (bf16[128,576]{0,1:T(8,128)(2,1)S(1)}, bf16[128,576]{0,1:T(8,128)(2,1)S(1)}, u32[]{:S(2)}, u32[]{:S(2)}) collective-permute-start(bf16[128,576]{0,1:T(8,128)(2,1)S(1)} %collective-permute-done.2), channel_id=1, source_target_pairs={{0,64},{8,72},{16,80},{24,88},{32,96},{40,104},{48,112},{56,120},{... | collective-permute-start | bytes 442376 | tf_op jit(solution)/shard_map/ppermute | solution.py:17
  199.9 25.9 %copy-start.38 = (bf16[128,32]{0,1:T(8,128)(2,1)}, bf16[128,32]{0,1:T(8,128)(2,1)S(1)}, u32[]{:S(2)}) copy-start(bf16[128,32]{0,1:T(8,128)(2,1)S(1)} %get-tuple-element.24) | copy-start | bytes 24580
  199.9 25.9 %copy-start.40 = (bf16[128,32]{0,1:T(8,128)(2,1)}, bf16[128,32]{0,1:T(8,128)(2,1)S(1)}, u32[]{:S(2)}) copy-start(bf16[128,32]{0,1:T(8,128)(2,1)S(1)} %get-tuple-element.25) | copy-start | bytes 24580
  212.6 12.7 %collective-permute-start.4 = (bf16[128,576]{0,1:T(8,128)(2,1)}, bf16[128,576]{0,1:T(8,128)(2,1)S(1)}, u32[]{:S(2)}, u32[]{:S(2)}) collective-permute-start(bf16[128,576]{0,1:T(8,128)(2,1)} %copy-done.25), channel_id=1, source_target_pairs={{0,64},{8,72},{16,80},{24,88},{32,96},{40,104},{48,112},{56,120},{... | collective-permute-start | bytes 442376 | tf_op jit(solution)/shard_map/ppermute | solution.py:17
  225.8 17.6 %copy-start.4 = (bf16[128,2048]{1,0:T(8,128)(2,1)}, bf16[128,2048]{1,0:T(8,128)(2,1)S(1)}, u32[]{:S(2)}) copy-start(bf16[128,2048]{1,0:T(8,128)(2,1)S(1)} %convolution_convert_fusion.2) | copy-start | bytes 1572868
  226.0 13.8 %collective-permute-start.5 = (bf16[128,576]{0,1:T(8,128)(2,1)S(1)}, bf16[128,576]{0,1:T(8,128)(2,1)S(1)}, u32[]{:S(2)}, u32[]{:S(2)}) collective-permute-start(bf16[128,576]{0,1:T(8,128)(2,1)S(1)} %collective-permute-done.4), channel_id=1, source_target_pairs={{0,64},{8,72},{16,80},{24,88},{32,96},{40,104},{48,112},{56,120},{... | collective-permute-start | bytes 442376 | tf_op jit(solution)/shard_map/ppermute | solution.py:17
  240.2 14.2 %copy-start.61 = (f32[32]{0:T(128)S(1)}, f32[32]{0:T(128)}, u32[]{:S(2)}) copy-start(f32[32]{0:T(128)} %multiply_power_fusion) | copy-start | bytes 388
  240.2 14.2 %copy-start.63 = (f32[128]{0:T(128)S(1)}, f32[128]{0:T(128)}, u32[]{:S(2)}) copy-start(f32[128]{0:T(128)} %get-tuple-element.10) | copy-start | bytes 1540
  240.3 14.2 %copy-start.64 = (f32[128]{0:T(128)S(1)}, f32[128]{0:T(128)}, u32[]{:S(2)}) copy-start(f32[128]{0:T(128)} %get-tuple-element.81) | copy-start | bytes 1540
  240.4 12.6 %collective-permute-start.6 = (bf16[128,576]{0,1:T(8,128)(2,1)S(1)}, bf16[128,576]{0,1:T(8,128)(2,1)S(1)}, u32[]{:S(2)}, u32[]{:S(2)}) collective-permute-start(bf16[128,576]{0,1:T(8,128)(2,1)S(1)} %collective-permute-done.5), channel_id=1, source_target_pairs={{0,64},{8,72},{16,80},{24,88},{32,96},{40,104},{48,112},{56,120},{... | collective-permute-start | bytes 442376 | tf_op jit(solution)/shard_map/ppermute | solution.py:17
  290.4 60.4 %copy-start.20 = (bf16[128,1536]{1,0:T(8,128)(2,1)S(1)}, bf16[128,1536]{1,0:T(8,128)(2,1)}, u32[]{:S(2)}) copy-start(bf16[128,1536]{1,0:T(8,128)(2,1)} %param.12) | copy-start | bytes 1179652
  290.4 605.5 %copy-start.1 = (bf16[512,2048]{1,0:T(8,128)(2,1)S(1)}, bf16[512,2048]{1,0:T(8,128)(2,1)}, u32[]{:S(2)}) copy-start(bf16[512,2048]{1,0:T(8,128)(2,1)} %param.15) | copy-start | bytes 6291460
  (57 other events, 226.8 us)
Sparse Core Ops, SparseCore 0:
  15.9 122.1 all-gather.2
  352.8 536.8 all-reduce.4
where the time goes:
time: 905 us; the launch traced here: 903 us
  waiting for transfers between devices  592 us (65%)
  blocking collectives  131 us (14%)
  local copies, waits for them, and re-layouts  66.2 us (7%)
  matrix products  47 us (5%)
  other arithmetic  30 us (3%)
  starting transfers between devices  20.1 us (2%)
  between operations  16.3 us (2%)
    psum x1, waiting for transfers between devices, body(): grad_qb, grad_qa = lax.psum((qb_term, qa_term), 'ctx')  535 us
    all_gather x1, blocking collectives, body(): all_offsets = lax.all_gather(block_starts, 'ctx', axis=0, tiled=True)  80.7 us
    ppermute x7, waiting for transfers between devices, passed_along(): return lax.ppermute(value, axis, pairs)  56.6 us
    psum x1, blocking collectives, body(): lax.psum(columns_contract(query_gradient, query_adapter_second), 'head')  50.8 us
    unnamed x181, local copies, waits for them, and re-layouts  26.2 us
    ppermute x7, starting transfers between devices, passed_along(): return lax.ppermute(value, axis, pairs)  20 us
  transfers between devices with their start and end apart: 9, of which 7 were waited for; matrix products, arithmetic and copies ran while one was open for 12% of the time, Pallas kernels for 0%

commit v1 on v0

--- a/solution.py
+++ b/solution.py
@@ -178,8 +178,8 @@
         .astype(jnp.bfloat16)
     )
     qb_term = contract_rows(query_rank_rows, query_gradient)
-    query_adapter_gradient = lax.psum(
-        columns_contract(query_gradient, query_adapter_second), "head"
+    query_adapter_gradient = jnp.sum(
+        lax.all_gather(columns_contract(query_gradient, query_adapter_second), "head"), axis=0
     ).astype(jnp.bfloat16)
     qa_term = contract_rows(query_latent_rows, query_adapter_gradient)
     grad_qb, grad_qa = lax.psum((qb_term, qa_term), "ctx")

time: 905 us -> 938 us (1.036)
  blocking collectives: 131 us -> 168 us
    all_gather x0 -> x1, blocking collectives: none -> 37.4 us  [body(): lax.all_gather(columns_contract(query_gradient, query_adapter_second), 'h...]
    unnamed x181 -> x182, local copies, waits for them, and re-layouts: 26.2 us -> 26.2 us
  transfers between devices with their start and end apart: 9 -> 9, of which waited for: 7 -> 7; matrix products, arithmetic and copies ran while one was open for 12% -> 11% of each run, Pallas kernels for 0% -> 0%
where the time goes in v1:
time: 938 us; the launch traced here: 936 us
  waiting for transfers between devices  591 us (63%)
  blocking collectives  168 us (18%)
  local copies, waits for them, and re-layouts  66.1 us (7%)
  matrix products  45.6 us (5%)
  other arithmetic  28.9 us (3%)
  starting transfers between devices  20.3 us (2%)
  between operations  16.4 us (2%)
    psum x1, waiting for transfers between devices, body(): grad_qb, grad_qa = lax.psum((qb_term, qa_term), 'ctx')  535 us
    all_gather x1, blocking collectives, body(): all_offsets = lax.all_gather(block_starts, 'ctx', axis=0, tiled=True)  80.7 us
    ppermute x7, waiting for transfers between devices, passed_along(): return lax.ppermute(value, axis, pairs)  55.7 us
    psum x1, blocking collectives, body(): output_rank_rows = lax.psum(output_partial_sum, 'head').astype(jnp.bfloat16)  50.2 us
    all_gather x1, blocking collectives, body(): lax.all_gather(columns_contract(query_gradient, query_adapter_second), 'h...  37.4 us
    unnamed x182, local copies, waits for them, and re-layouts  26.2 us
    ppermute x7, starting transfers between devices, passed_along(): return lax.ppermute(value, axis, pairs)  20.2 us
  transfers between devices with their start and end apart: 9, of which 7 were waited for; matrix products, arithmetic and copies ran while one was open for 11% of the time, Pallas kernels for 0%

profile of v1, /device:TPU:1, one launch (start us, length us, event | category | flops | bytes accessed | tf_op | source)
XLA Modules:
  0.0 936.4 jit_solution(12284490339084800362)
XLA Ops:
  7.3 8.5 collective-permute-start
  24.4 80.7 %all-gather.1 = s32[64,1,2]{2,1,0:T(1,128)} all-gather(s32[1,1,2]{2,1,0:T(1,128)S(1)} %bitcast.215), channel_id=1, replica_groups=mesh['ctx'=64,'head'=8] {'ctx'}, dimensions={0}, use_global_device_ids=true | all-gather | bytes 520 | tf_op jit(solution)/shard_map/all_gather | solution.py:98
  123.6 2.0 fusion.62
  150.4 1.9 constant_dynamic-update-slice_fusion.6
  152.4 1.9 collective-permute-start.1
  154.3 2.0 fusion.60
  156.2 10.1 %collective-permute-done.1 = bf16[128,576]{0,1:T(8,128)(2,1)S(1)} collective-permute-done((bf16[128,576]{0,1:T(8,128)(2,1)}, bf16[128,576]{0,1:T(8,128)(2,1)S(1)}, u32[]{:S(2)}, u32[]{:S(2)}) %collective-permute-start.1) | collective-permute-done | bytes 147488 | tf_op jit(solution)/shard_map/ppermute | solution.py:17
  168.0 1.9 collective-permute-start.2
  169.9 12.2 %collective-permute-done.2 = bf16[128,576]{0,1:T(8,128)(2,1)S(1)} collective-permute-done((bf16[128,576]{0,1:T(8,128)(2,1)S(1)}, bf16[128,576]{0,1:T(8,128)(2,1)S(1)}, u32[]{:S(2)}, u32[]{:S(2)}) %collective-permute-start.2) | collective-permute-done | bytes 147488 | tf_op jit(solution)/shard_map/ppermute | solution.py:17
  183.9 1.9 collective-permute-start.3
  185.8 10.5 %collective-permute-done.3 = bf16[128,576]{0,1:T(8,128)(2,1)S(1)} collective-permute-done((bf16[128,576]{0,1:T(8,128)(2,1)S(1)}, bf16[128,576]{0,1:T(8,128)(2,1)S(1)}, u32[]{:S(2)}, u32[]{:S(2)}) %collective-permute-start.3) | collective-permute-done | bytes 147488 | tf_op jit(solution)/shard_map/ppermute | solution.py:17
  206.5 1.9 concatenate.151
  210.3 1.9 concatenate.155
  212.2 1.9 collective-permute-start.4
  214.1 1.9 constant_dynamic-update-slice_fusion.5
  216.1 2.0 constant_dynamic-update-slice_fusion.4
  218.0 1.9 constant_dynamic-update-slice_fusion.3
  219.9 1.9 fusion.54
  221.9 3.0 collective-permute-done.4
  225.5 1.9 collective-permute-start.5
  228.5 10.4 %collective-permute-done.5 = bf16[128,576]{0,1:T(8,128)(2,1)S(1)} collective-permute-done((bf16[128,576]{0,1:T(8,128)(2,1)S(1)}, bf16[128,576]{0,1:T(8,128)(2,1)S(1)}, u32[]{:S(2)}, u32[]{:S(2)}) %collective-permute-start.5) | collective-permute-done | bytes 147488 | tf_op jit(solution)/shard_map/ppermute | solution.py:17
  239.6 2.1 collective-permute-start.6
  242.8 9.4 %collective-permute-done.6 = bf16[128,576]{0,1:T(8,128)(2,1)S(1)} collective-permute-done((bf16[128,576]{0,1:T(8,128)(2,1)S(1)}, bf16[128,576]{0,1:T(8,128)(2,1)S(1)}, u32[]{:S(2)}, u32[]{:S(2)}) %collective-permute-start.6) | collective-permute-done | bytes 147488 | tf_op jit(solution)/shard_map/ppermute | solution.py:17
  261.6 2.5 slice.337
  270.0 1.9 fusion.188
  274.8 50.2 %psum.31 = bf16[128,32]{0,1:T(8,128)(2,1)S(1)} all-reduce(f32[128,32]{0,1:T(8,128)S(1)} %fusion.201), channel_id=1, replica_groups=mesh['ctx'=64,'head'=8] {'head'}, use_global_device_ids=true, to_apply=%region_7.8 | all-reduce | flops 4096 | bytes 24576 | tf_op jit(solution)/shard_map/psum | solution.py:150
  326.8 3.3 fusion.197
  330.4 2.7 fusion.16
  333.1 6.0 fusion.42
  339.2 7.4 fusion.43
  347.8 37.4 %all-gather = f32[1024,32]{0,1:T(8,128)S(1)} all-gather(f32[128,32]{0,1:T(8,128)S(1)} %fusion.200), channel_id=2, replica_groups=mesh['ctx'=64,'head'=8] {'head'}, dimensions={0}, use_global_device_ids=true | all-gather | bytes 147456 | tf_op jit(solution)/shard_map/all_gather | solution.py:182
  388.1 535.2 %all-reduce.4.cloned.1.call-done = (f32[1536,32]{0,1:T(8,128)}, f32[32,1536]{1,0:T(8,128)}, f32[1024,32]{0,1:T(8,128)}, f32[32,2560]{1,0:T(8,128)}) async-done(((f32[1536,32]{0,1:T(8,128)}, f32[32,1536]{1,0:T(8,128)}, f32[1024,32]{0,1:T(8,128)}, f32[32,2560]{1,0:T(8,128)}), (f32[1536,32]{0,1:T(8,128)}, f32[32,1536]{1,0:T(8,128)}, f32[1024,32]{0,1:T(8,128)}, ...) | async-done | bytes 851984 | tf_op jit(solution)/shard_map/psum | solution.py:185
  (300 shorter events, 99.4 us)
Async XLA Ops:
  7.2 16.5 %copy-start.62 = (s32[1,2]{1,0:T(1,128)S(1)}, s32[1,2]{1,0:T(1,128)}, u32[]{:S(2)}) copy-start(s32[1,2]{1,0:T(1,128)} %param.14) | copy-start | bytes 28
  7.2 319.5 %all-gather.4.cloned.1.call-start = ((), (), s32[]{:S(2)}) async-start(), calls=%async_computation | async-start | bytes 5324800 | tf_op jit(solution)/shard_map/all_gather | solution.py:159
  7.3 128.0 %collective-permute-start = (bf16[128,576]{0,1:T(8,128)(2,1)}, bf16[128,576]{0,1:T(8,128)(2,1)}, u32[]{:S(2)}, u32[]{:S(2)}) collective-permute-start(bf16[128,576]{0,1:T(8,128)(2,1)} %param.13), channel_id=1, source_target_pairs={{0,64},{8,72},{16,80},{24,88},{32,96},{40,104},{48,112},{56,120},{... | collective-permute-start | bytes 442376 | tf_op jit(solution)/shard_map/ppermute | solution.py:17
  15.8 907.5 %all-reduce.4.cloned.1.call-start = ((), (), s32[]{:S(2)}) async-start(), calls=%async_computation.1 | async-start | bytes 1703936 | tf_op jit(solution)/shard_map/psum | solution.py:185
  18.0 113.0 %copy-start.2 = (bf16[128,2560]{1,0:T(8,128)(2,1)S(1)}, bf16[128,2560]{1,0:T(8,128)(2,1)}, u32[]{:S(2)}) copy-start(bf16[128,2560]{1,0:T(8,128)(2,1)} %param.21) | copy-start | bytes 1966084
  108.9 19.7 %copy-start.70 = (s32[64]{0:T(128)}, s32[64]{0:T(128)S(1)}, u32[]{:S(2)}) copy-start(s32[64]{0:T(128)S(1)} %iota_add_fusion.14) | copy-start | bytes 772
  109.5 19.1 %copy-start.71 = (s32[64]{0:T(128)}, s32[64]{0:T(128)S(1)}, u32[]{:S(2)}) copy-start(s32[64]{0:T(128)S(1)} %iota_add_fusion.15) | copy-start | bytes 772
  110.8 17.8 %copy-start.78 = (s32[64]{0:T(128)}, s32[64]{0:T(128)S(1)}, u32[]{:S(2)}) copy-start(s32[64]{0:T(128)S(1)} %iota_add_fusion.2) | copy-start | bytes 772
  111.5 17.1 %copy-start.79 = (s32[64]{0:T(128)}, s32[64]{0:T(128)S(1)}, u32[]{:S(2)}) copy-start(s32[64]{0:T(128)S(1)} %iota_add_fusion.3) | copy-start | bytes 772
  112.8 15.9 %copy-start.72 = (s32[64]{0:T(128)}, s32[64]{0:T(128)S(1)}, u32[]{:S(2)}) copy-start(s32[64]{0:T(128)S(1)} %iota_add_fusion.6) | copy-start | bytes 772
  113.4 15.2 %copy-start.73 = (s32[64]{0:T(128)}, s32[64]{0:T(128)S(1)}, u32[]{:S(2)}) copy-start(s32[64]{0:T(128)S(1)} %iota_add_fusion.7) | copy-start | bytes 772
  140.5 26.2 %copy-start.32 = (bf16[128,32]{0,1:T(8,128)(2,1)}, bf16[128,32]{0,1:T(8,128)(2,1)S(1)}, u32[]{:S(2)}) copy-start(bf16[128,32]{0,1:T(8,128)(2,1)S(1)} %get-tuple-element.28) | copy-start | bytes 24580
  140.5 26.2 %copy-start.34 = (bf16[128,32]{0,1:T(8,128)(2,1)}, bf16[128,32]{0,1:T(8,128)(2,1)S(1)}, u32[]{:S(2)}) copy-start(bf16[128,32]{0,1:T(8,128)(2,1)S(1)} %get-tuple-element.29) | copy-start | bytes 24580
  152.4 13.9 %collective-permute-start.1 = (bf16[128,576]{0,1:T(8,128)(2,1)}, bf16[128,576]{0,1:T(8,128)(2,1)S(1)}, u32[]{:S(2)}, u32[]{:S(2)}) collective-permute-start(bf16[128,576]{0,1:T(8,128)(2,1)} %collective-permute-done), channel_id=1, source_target_pairs={{0,64},{8,72},{16,80},{24,88},{32,96},{40,104},{48,112},{56,120},{... | collective-permute-start | bytes 442376 | tf_op jit(solution)/shard_map/ppermute | solution.py:17
  166.8 17.1 %copy-start.5 = (bf16[128,2048]{1,0:T(8,128)(2,1)}, bf16[128,2048]{1,0:T(8,128)(2,1)S(1)}, u32[]{:S(2)}) copy-start(bf16[128,2048]{1,0:T(8,128)(2,1)S(1)} %convolution_convert_fusion.5) | copy-start | bytes 1572868
  168.0 14.2 %collective-permute-start.2 = (bf16[128,576]{0,1:T(8,128)(2,1)S(1)}, bf16[128,576]{0,1:T(8,128)(2,1)S(1)}, u32[]{:S(2)}, u32[]{:S(2)}) collective-permute-start(bf16[128,576]{0,1:T(8,128)(2,1)S(1)} %collective-permute-done.1), channel_id=1, source_target_pairs={{0,64},{8,72},{16,80},{24,88},{32,96},{40,104},{48,112},{56,120},{... | collective-permute-start | bytes 442376 | tf_op jit(solution)/shard_map/ppermute | solution.py:17
  182.7 15.8 %copy-start.60 = (f32[32]{0:T(128)S(1)}, f32[32]{0:T(128)}, u32[]{:S(2)}) copy-start(f32[32]{0:T(128)} %multiply_power_fusion) | copy-start | bytes 388
  182.7 15.8 %copy-start.66 = (f32[128]{0:T(128)S(1)}, f32[128]{0:T(128)}, u32[]{:S(2)}) copy-start(f32[128]{0:T(128)} %get-tuple-element.77) | copy-start | bytes 1540
  182.7 15.8 %copy-start.67 = (f32[128]{0:T(128)S(1)}, f32[128]{0:T(128)}, u32[]{:S(2)}) copy-start(f32[128]{0:T(128)} %get-tuple-element.78) | copy-start | bytes 1540
  182.7 15.8 %copy-start.77 = (f32[128]{0:T(128)S(1)}, f32[128]{0:T(128)}, u32[]{:S(2)}) copy-start(f32[128]{0:T(128)} %add_convert_fusion.6) | copy-start | bytes 1540
  183.9 12.5 %collective-permute-start.3 = (bf16[128,576]{0,1:T(8,128)(2,1)S(1)}, bf16[128,576]{0,1:T(8,128)(2,1)S(1)}, u32[]{:S(2)}, u32[]{:S(2)}) collective-permute-start(bf16[128,576]{0,1:T(8,128)(2,1)S(1)} %collective-permute-done.2), channel_id=1, source_target_pairs={{0,64},{8,72},{16,80},{24,88},{32,96},{40,104},{48,112},{56,120},{... | collective-permute-start | bytes 442376 | tf_op jit(solution)/shard_map/ppermute | solution.py:17
  199.4 25.9 %copy-start.38 = (bf16[128,32]{0,1:T(8,128)(2,1)}, bf16[128,32]{0,1:T(8,128)(2,1)S(1)}, u32[]{:S(2)}) copy-start(bf16[128,32]{0,1:T(8,128)(2,1)S(1)} %get-tuple-element.22) | copy-start | bytes 24580
  199.4 26.0 %copy-start.40 = (bf16[128,32]{0,1:T(8,128)(2,1)}, bf16[128,32]{0,1:T(8,128)(2,1)S(1)}, u32[]{:S(2)}) copy-start(bf16[128,32]{0,1:T(8,128)(2,1)S(1)} %get-tuple-element.23) | copy-start | bytes 24580
  212.2 12.7 %collective-permute-start.4 = (bf16[128,576]{0,1:T(8,128)(2,1)}, bf16[128,576]{0,1:T(8,128)(2,1)S(1)}, u32[]{:S(2)}, u32[]{:S(2)}) collective-permute-start(bf16[128,576]{0,1:T(8,128)(2,1)} %copy-done.25), channel_id=1, source_target_pairs={{0,64},{8,72},{16,80},{24,88},{32,96},{40,104},{48,112},{56,120},{... | collective-permute-start | bytes 442376 | tf_op jit(solution)/shard_map/ppermute | solution.py:17
  225.4 17.4 %copy-start.4 = (bf16[128,2048]{1,0:T(8,128)(2,1)}, bf16[128,2048]{1,0:T(8,128)(2,1)S(1)}, u32[]{:S(2)}) copy-start(bf16[128,2048]{1,0:T(8,128)(2,1)S(1)} %convolution_convert_fusion.2) | copy-start | bytes 1572868
  225.5 13.4 %collective-permute-start.5 = (bf16[128,576]{0,1:T(8,128)(2,1)S(1)}, bf16[128,576]{0,1:T(8,128)(2,1)S(1)}, u32[]{:S(2)}, u32[]{:S(2)}) collective-permute-start(bf16[128,576]{0,1:T(8,128)(2,1)S(1)} %collective-permute-done.4), channel_id=1, source_target_pairs={{0,64},{8,72},{16,80},{24,88},{32,96},{40,104},{48,112},{56,120},{... | collective-permute-start | bytes 442376 | tf_op jit(solution)/shard_map/ppermute | solution.py:17
  239.4 14.2 %copy-start.61 = (f32[32]{0:T(128)S(1)}, f32[32]{0:T(128)}, u32[]{:S(2)}) copy-start(f32[32]{0:T(128)} %multiply_power_fusion) | copy-start | bytes 388
  239.4 14.2 %copy-start.63 = (f32[128]{0:T(128)S(1)}, f32[128]{0:T(128)}, u32[]{:S(2)}) copy-start(f32[128]{0:T(128)} %get-tuple-element.8) | copy-start | bytes 1540
  239.6 12.5 %collective-permute-start.6 = (bf16[128,576]{0,1:T(8,128)(2,1)S(1)}, bf16[128,576]{0,1:T(8,128)(2,1)S(1)}, u32[]{:S(2)}, u32[]{:S(2)}) collective-permute-start(bf16[128,576]{0,1:T(8,128)(2,1)S(1)} %collective-permute-done.5), channel_id=1, source_target_pairs={{0,64},{8,72},{16,80},{24,88},{32,96},{40,104},{48,112},{56,120},{... | collective-permute-start | bytes 442376 | tf_op jit(solution)/shard_map/ppermute | solution.py:17
  271.9 53.0 %copy-start.31 = (bf16[128,32]{0,1:T(8,128)(2,1)S(1)}, bf16[128,32]{0,1:T(8,128)(2,1)}, u32[]{:S(2)}) copy-start(bf16[128,32]{0,1:T(8,128)(2,1)} %convolution_convert_fusion.8) | copy-start | bytes 24580
  339.1 46.2 %copy-start.20 = (bf16[128,1536]{1,0:T(8,128)(2,1)S(1)}, bf16[128,1536]{1,0:T(8,128)(2,1)}, u32[]{:S(2)}) copy-start(bf16[128,1536]{1,0:T(8,128)(2,1)} %param.12) | copy-start | bytes 1179652
  339.1 590.4 %copy-start.1 = (bf16[512,2048]{1,0:T(8,128)(2,1)S(1)}, bf16[512,2048]{1,0:T(8,128)(2,1)}, u32[]{:S(2)}) copy-start(bf16[512,2048]{1,0:T(8,128)(2,1)} %param.15) | copy-start | bytes 6291460
  (57 other events, 235.3 us)
Sparse Core Ops, SparseCore 0:
  15.9 122.0 all-gather.3
  386.3 536.9 all-reduce.3
